TPU v7x, 128 devices: a whole 4x4x4 slice. The times are simulated.
128 devices in a mesh: ctx: 32 (over z, x, core), head: 4 (over y).
Axes of the slice: x: 4, y: 4, z: 4, core: 2. Of those that a mesh axis runs over, the one named last changes fastest.
Arguments:
- queries: bfloat16 [16384, 2048], P('ctx', 'head'), may hold values from -6 to 6
- key_rows: bfloat16 [16384, 2048], P('ctx', 'head'), may hold values from -6 to 6
- value_rows: bfloat16 [16384, 2048], P('ctx', 'head'), may hold values from -6 to 6
- targets: bfloat16 [16384, 512], P('ctx'), may hold values from -2.5 to 2.5
- readout: bfloat16 [512, 4096], P(None, 'head'), may hold values from -0.25 to 0.25
- retain: float32 [32, 16], P('ctx', 'head'), may hold values from 0.3 to 1
- learn_rate: float32 [32, 16], P('ctx', 'head'), may hold values from 0.01 to 0.1
- allowed: int32 [32, 2], replicated, may hold values 0 or 1
- positions: int32 [32, 128], P('ctx'), may hold values from 0 to 511, as said below
- grad_out: bfloat16 [16384, 2048], P('ctx', 'head'), may hold values from -6 to 6
Outputs:
- grad_queries: float32 [16384, 2048], P('ctx', 'head')
- grad_keys: float32 [16384, 2048], P('ctx', 'head')
- grad_values: float32 [16384, 2048], P('ctx', 'head')
- grad_targets: float32 [16384, 512], P('ctx', 'head')
- grad_readout: float32 [512, 4096], P('ctx', 'head')
Inputs may be any that keep to these rules, and one draw needn't show every extreme that they name: The 128 positions of a segment are distinct, ascending, and include 0 and 511.
All inputs are finite; a program needn't handle non-finite values.
Results may differ from a plain program's by a relative error of at most 0.0081.
Values may be sent and summed in bfloat16 or wider, within the bound.
A program may use at most 192 MiB of HBM per device.

v0:
```python
from functools import reduce
import jax
import jax.numpy as jnp
from jax import lax
from jax.sharding import PartitionSpec as P

masked_score = -1e30
highest = lax.Precision.HIGHEST


def entering(value, axis, join, neutral, backward):
    count, mine = (lax.axis_size(axis), lax.axis_index(axis))
    pieces = jax.tree.map(lambda part: lax.all_gather(part, axis), value)
    if backward:
        pieces = jax.tree.map(lambda part: part[::-1], pieces)
        mine = count - 1 - mine
    subtotal = jax.tree.map(
        lambda part, zero: jnp.full_like(part, 0) + jnp.asarray(zero, part.dtype), value, neutral
    )

    def turn(position, subtotal):
        longer = join(subtotal, jax.tree.map(lambda part: part[position], pieces))
        return jax.tree.map(lambda new, old: jnp.where(position < mine, new, old), longer, subtotal)

    return lax.fori_loop(0, count - 1, turn, subtotal)


def shifted_2(value, axis, steps):
    count = lax.axis_size(axis)
    leading, last = (max(0, -steps), min(count, count - steps))
    return lax.ppermute(value, axis, [(source, source + steps) for source in range(leading, last)])


def compose(earlier_map, later_map):
    linear_part = jnp.einsum("hab,hbc->hac", later_map[0], earlier_map[0], precision=highest)
    shift_part = (
        jnp.einsum("hab,hbf->haf", later_map[0], earlier_map[1], precision=highest) + later_map[1]
    )
    return (linear_part, shift_part)


def score_block(left_rows, right_rows, score_scale):
    return (
        lax.dot_general(
            left_rows, right_rows, (((1,), (1,)), ((), ())), preferred_element_type=jnp.float32
        )
        * score_scale
    )


def gated_scores(left_rows, right_rows, usable, score_scale):
    return jnp.where(usable, score_block(left_rows, right_rows, score_scale), masked_score)


def scores_grad(cotangent, values_tile, probs_tile, row_delta):
    grad_probs = lax.dot_general(
        cotangent, values_tile, (((1,), (1,)), ((), ())), preferred_element_type=jnp.float32
    )
    return (probs_tile * (grad_probs - row_delta)).astype(jnp.bfloat16)


def block_all(
    queries_tile, cotangent, keys_tile, values_tile, probs_tile, probs_low, row_delta, score_scale
):
    grad_scores = scores_grad(cotangent, values_tile, probs_tile, row_delta)
    grad_rows = jnp.dot(grad_scores, keys_tile, preferred_element_type=jnp.float32) * score_scale
    grad_cols = (
        lax.dot_general(
            grad_scores, queries_tile, (((0,), (0,)), ((), ())), preferred_element_type=jnp.float32
        )
        * score_scale
    )
    grad_vals = lax.dot_general(
        probs_low, cotangent, (((0,), (0,)), ((), ())), preferred_element_type=jnp.float32
    )
    return (grad_rows, grad_cols, grad_vals)


def far_all(
    queries_tile, cotangent, keys_tile, values_tile, probs_tile, probs_low, row_delta, score_scale
):
    return block_all(
        queries_tile,
        cotangent,
        keys_tile,
        values_tile,
        probs_tile,
        probs_low,
        row_delta,
        score_scale,
    )


def on_device(
    queries,
    key_rows,
    value_rows,
    targets,
    readout,
    retain,
    learn_rate,
    allowed,
    positions,
    grad_out,
):
    seg_len = queries.shape[0]
    local_heads = retain.shape[1]
    head_width = queries.shape[1] // local_heads
    mem_rows = positions.shape[1]
    block_reach = allowed.shape[1]
    segment = lax.axis_index("ctx")
    score_scale = head_width ** (-0.5)
    key_heads = key_rows.reshape(seg_len, local_heads, head_width)
    key_gram = jnp.einsum("sha,shb->hab", key_heads, key_heads, preferred_element_type=jnp.float32)
    identity_block = jnp.eye(head_width, dtype=jnp.float32)
    decay_map = (
        retain[0][:, None, None] * identity_block
        - (learn_rate[0] / seg_len)[:, None, None] * key_gram
    )
    write_map = (
        jnp.einsum("sha,sf->haf", key_heads, targets, preferred_element_type=jnp.float32) / seg_len
    )
    neutral = (jnp.broadcast_to(identity_block, decay_map.shape), jnp.zeros_like(write_map))
    memory_in = entering((decay_map, write_map), "ctx", compose, neutral, False)[1]
    pick_rows = positions[0]
    picked = (
        jnp.take(queries, pick_rows, axis=0)
        .astype(jnp.float32)
        .reshape(mem_rows, local_heads, head_width)
    )
    partial_read = jnp.einsum("nha,haf->nf", picked, memory_in, precision=highest)
    hidden_read = lax.psum(partial_read, "head").astype(jnp.bfloat16)
    memory_tokens = jnp.dot(hidden_read, readout, preferred_element_type=jnp.float32).reshape(
        mem_rows, local_heads, 2, head_width
    )
    memory_keys = memory_tokens[:, :, 0].astype(jnp.bfloat16)
    memory_values = memory_tokens[:, :, 1].astype(jnp.bfloat16)
    remote = []
    for offset in range(1, block_reach + 1):
        shifted = shifted_2((key_rows, value_rows), "ctx", offset)
        usable = (allowed[segment, offset - 1] == 1) & (segment >= offset)
        remote.append((shifted[0], shifted[1], usable))
    causal = lax.broadcasted_iota(jnp.int32, (seg_len, seg_len), 0) >= lax.broadcasted_iota(
        jnp.int32, (seg_len, seg_len), 1
    )
    rows_list, keys_own, values_own = ([], [], [])
    mem_key_grads, mem_value_grads = ([], [])
    far_keys = [[] for offset in range(block_reach)]
    far_values = [[] for offset in range(block_reach)]
    max_list, total_list, delta_list = ([], [], [])
    for head_index in range(local_heads):
        columns = slice(head_index * head_width, (head_index + 1) * head_width)
        queries_tile = queries[:, columns]
        cotangent = grad_out[:, columns]
        key_collection = [memory_keys[:, head_index], key_rows[:, columns]] + [
            remote_item[0][:, columns] for remote_item in remote
        ]
        values_list = [memory_values[:, head_index], value_rows[:, columns]] + [
            remote_item[1][:, columns] for remote_item in remote
        ]
        score_list = [
            score_block(queries_tile, key_collection[0], score_scale),
            jnp.where(
                causal, score_block(queries_tile, key_collection[1], score_scale), masked_score
            ),
        ]
        score_list = score_list + [
            gated_scores(
                queries_tile, key_collection[2 + tile_index], remote[tile_index][2], score_scale
            )
            for tile_index in range(block_reach)
        ]
        row_max = reduce(
            jnp.maximum, [jnp.max(score_tile, axis=1, keepdims=True) for score_tile in score_list]
        )
        exp_tiles = [jnp.exp(score_tile - row_max) for score_tile in score_list]
        row_total = reduce(
            jnp.add, [jnp.sum(exp_tile, axis=1, keepdims=True) for exp_tile in exp_tiles]
        )
        probs_list = [exp_tile / row_total for exp_tile in exp_tiles]
        probs_lows = [probs_tile.astype(jnp.bfloat16) for probs_tile in probs_list]
        attended = reduce(
            jnp.add,
            [
                jnp.dot(low_tile, value_tile, preferred_element_type=jnp.float32)
                for low_tile, value_tile in zip(probs_lows, values_list)
            ],
        )
        row_delta = jnp.sum(cotangent.astype(jnp.float32) * attended, axis=1, keepdims=True)
        mem_grads = block_all(
            queries_tile,
            cotangent,
            key_collection[0],
            values_list[0],
            probs_list[0],
            probs_lows[0],
            row_delta,
            score_scale,
        )
        own_grads = block_all(
            queries_tile,
            cotangent,
            key_collection[1],
            values_list[1],
            probs_list[1],
            probs_lows[1],
            row_delta,
            score_scale,
        )
        grad_rows = mem_grads[0] + own_grads[0]
        for tile_index in range(block_reach):
            far_grads = far_all(
                queries_tile,
                cotangent,
                key_collection[2 + tile_index],
                values_list[2 + tile_index],
                probs_list[2 + tile_index],
                probs_lows[2 + tile_index],
                row_delta,
                score_scale,
            )
            grad_rows = grad_rows + far_grads[0]
            far_keys[tile_index].append(far_grads[1])
            far_values[tile_index].append(far_grads[2])
        rows_list.append(grad_rows)
        keys_own.append(own_grads[1])
        values_own.append(own_grads[2])
        mem_key_grads.append(mem_grads[1])
        mem_value_grads.append(mem_grads[2])
        max_list.append(row_max)
        total_list.append(row_total)
        delta_list.append(row_delta)
    grad_queries = jnp.concatenate(rows_list, axis=1)
    key_total = jnp.concatenate(keys_own, axis=1)
    value_total = jnp.concatenate(values_own, axis=1)
    for offset in range(1, block_reach + 1):
        returned = shifted_2(
            (
                jnp.concatenate(far_keys[offset - 1], axis=1),
                jnp.concatenate(far_values[offset - 1], axis=1),
            ),
            "ctx",
            -offset,
        )
        key_total = key_total + returned[0]
        value_total = value_total + returned[1]
    grad_memory = jnp.stack(
        [jnp.stack(mem_key_grads, axis=1), jnp.stack(mem_value_grads, axis=1)], axis=2
    )
    grad_memory = grad_memory.reshape(mem_rows, local_heads * 2 * head_width).astype(jnp.bfloat16)
    readout_term = lax.dot_general(
        hidden_read, grad_memory, (((0,), (0,)), ((), ())), preferred_element_type=jnp.float32
    )
    grad_readout = lax.psum_scatter(readout_term, "ctx", scatter_dimension=0, tiled=True)
    hidden_term = lax.dot_general(
        grad_memory, readout, (((1,), (1,)), ((), ())), preferred_element_type=jnp.float32
    )
    grad_hidden = lax.psum(hidden_term, "head")
    grad_picked = jnp.einsum("nf,haf->nha", grad_hidden, memory_in, precision=highest).reshape(
        mem_rows, local_heads * head_width
    )
    grad_state = jnp.einsum("nha,nf->haf", picked, grad_hidden, precision=highest)
    grad_queries = grad_queries + jnp.zeros_like(grad_queries).at[pick_rows].add(grad_picked)
    flipped = jnp.swapaxes(decay_map, 1, 2)
    grad_after = entering((flipped, grad_state), "ctx", compose, neutral, True)[1]
    grad_decay = jnp.einsum("haf,hbf->hab", grad_after, memory_in, precision=highest)
    symmetric = grad_decay + jnp.swapaxes(grad_decay, 1, 2)
    keys_wide = key_heads.astype(jnp.float32)
    key_memory = (
        jnp.einsum("sf,haf->sha", targets.astype(jnp.float32), grad_after, precision=highest)
        / seg_len
    )
    key_memory = key_memory - (learn_rate[0] / seg_len)[None, :, None] * jnp.einsum(
        "sha,hab->shb", keys_wide, symmetric, precision=highest
    )
    key_total = key_total + key_memory.reshape(seg_len, local_heads * head_width)
    target_term = jnp.einsum("sha,haf->sf", keys_wide, grad_after, precision=highest) / seg_len
    grad_targets = lax.psum_scatter(target_term, "head", scatter_dimension=1, tiled=True)
    return (grad_queries, key_total, value_total, grad_targets, grad_readout)


def solution(mesh):
    return jax.shard_map(
        on_device,
        mesh=mesh,
        in_specs=(
            P("ctx", "head"),
            P("ctx", "head"),
            P("ctx", "head"),
            P("ctx", None),
            P(None, "head"),
            P("ctx", "head"),
            P("ctx", "head"),
            P(),
            P("ctx", None),
            P("ctx", "head"),
        ),
        out_specs=(
            P("ctx", "head"),
            P("ctx", "head"),
            P("ctx", "head"),
            P("ctx", "head"),
            P("ctx", "head"),
        ),
        check_vma=False,
    )
```

profile of v0, /device:TPU:0, one launch (start us, length us, event | category | flops | bytes accessed | tf_op | source)
XLA Modules:
  0.0 802.2 jit_solution(9045116034539921850)
XLA Ops:
  17.8 4.3 collective-permute-start.3
  24.4 3.1 collective-permute-start.1
  27.5 3.7 collective-permute-start
  45.8 2.7 fusion.313
  48.5 2.7 fusion.317
  51.3 2.7 fusion.311
  60.6 2.8 fusion.310
  63.4 2.8 fusion.314
  66.2 2.7 fusion.318
  71.6 21.3 %all-gather.9.cloned.1.call-done = f32[128,128,128]{2,1,0:T(8,128)} async-done(((f32[4,128,128]{2,1,0:T(8,128)}), f32[128,128,128]{2,1,0:T(8,128)}) %all-gather.9.cloned.1.call-update) | async-done | bytes 8388624 | tf_op jit(solution)/shard_map/all_gather | solution.py:13
  92.9 115.6 %all-gather.11.cloned.1.call-done = f32[128,128,512]{2,1,0:T(8,128)} async-done(((f32[4,128,512]{2,1,0:T(8,128)}), f32[128,128,512]{2,1,0:T(8,128)}) %all-gather.11.cloned.1.call-update) | async-done | bytes 33554448 | tf_op jit(solution)/shard_map/all_gather | solution.py:13
  208.5 78.0 %while.28 = (s32[]{:T(128)}, f32[4,128,512]{2,1,0:T(8,128)S(1)}, s32[]{:T(128)}, f32[32,4,128,128]{3,2,1,0:T(8,128)}, f32[32,4,128,512]{3,2,1,0:T(8,128)}, /*index=5*/s32[]{:T(128)}, s32[]{:T(128)}) while((s32[]{:T(128)}, f32[4,128,512]{2,1,0:T(8,128)S(1)}, s32[]{:T(128)}, f32[32,4,128,128]{3,2,1,0:T(8,128)}, ...), condition=%wide.region_1.2_spmd.clone, body=%wide.region_0.1_spmd.clone.sunk | while | flops 403701760 | bytes 6556263 | solution.py:25
  287.8 21.1 %all-reduce.4 = bf16[128,512]{1,0:T(8,128)(2,1)S(1)} all-reduce(f32[128,512]{1,0:T(8,128)} %convolution_bitcast_fusion.1), channel_id=1, replica_groups=mesh['ctx'=32,'head'=4] {'head'}, use_global_device_ids=true, to_apply=%region_2.3 | all-reduce | flops 65536 | bytes 393216 | tf_op jit(solution)/shard_map/psum | solution.py:132
  341.4 37.8 %all-reduce.3.cloned.1.call-done = f32[128,512]{1,0:T(8,128)} async-done(((f32[128,512]{1,0:T(8,128)}), f32[128,512]{1,0:T(8,128)}) %all-reduce.3.cloned.1.call-update) | async-done | bytes 262160 | tf_op jit(solution)/shard_map/psum | solution.py:258
  382.3 52.2 %all-gather.13.cloned.1.call-done = f32[128,128,128]{2,1,0:T(8,128)} async-done(((f32[4,128,128]{2,1,0:T(8,128)}), f32[128,128,128]{2,1,0:T(8,128)}) %all-gather.13.cloned.1.call-update) | async-done | bytes 8388624 | tf_op jit(solution)/shard_map/all_gather | solution.py:13
  434.6 7.9 rev.6
  496.5 84.6 %all-gather.15.cloned.1.call-done = f32[128,128,512]{2,1,0:T(8,128)} async-done(((f32[4,128,512]{2,1,0:T(8,128)}), f32[128,128,512]{2,1,0:T(8,128)}) %all-gather.15.cloned.1.call-update) | async-done | bytes 33554448 | tf_op jit(solution)/shard_map/all_gather | solution.py:13
  581.2 23.4 %rev.7 = f32[32,4,128,512]{3,2,1,0:T(8,128)} reverse(f32[32,4,128,512]{3,2,1,0:T(8,128)} %bitcast.227), dimensions={0} | reverse | bytes 67108864 | tf_op jit(solution)/shard_map/rev | solution.py:15
  604.6 78.1 %while.29 = (s32[]{:T(128)}, f32[4,128,512]{2,1,0:T(8,128)S(1)}, s32[]{:T(128)}, f32[32,4,128,128]{3,2,1,0:T(8,128)}, f32[32,4,128,512]{3,2,1,0:T(8,128)}, /*index=5*/s32[]{:T(128)}, s32[]{:T(128)}) while((s32[]{:T(128)}, f32[4,128,512]{2,1,0:T(8,128)S(1)}, s32[]{:T(128)}, f32[32,4,128,128]{3,2,1,0:T(8,128)}, ...), condition=%wide.region_42.43_spmd.clone, body=%wide.region_41.42_spmd.clone.sunk | while | flops 403701760 | bytes 6556263 | solution.py:25
  682.8 4.0 fusion.42
  721.2 3.7 scatter_fusion
  724.9 3.1 fusion.97
  736.5 3.5 collective-permute-done.5
  745.4 49.8 %reduce-scatter.5.cloned.1.call-done = f32[16,1024]{1,0:T(8,128)} async-done(((f32[512,1024]{1,0:T(8,128)}), f32[16,1024]{1,0:T(8,128)}) %reduce-scatter.5.cloned.1.call-update) | async-done | bytes 65552 | tf_op jit(solution)/shard_map/reduce_scatter | solution.py:254
  (522 shorter events, 326.6 us)
Async XLA Ops:
  7.2 301.8 %copy-start = (bf16[512,1024]{1,0:T(8,128)(2,1)S(1)}, bf16[512,1024]{1,0:T(8,128)(2,1)}, u32[]{:S(2)}) copy-start(bf16[512,1024]{1,0:T(8,128)(2,1)} %param.18) | copy-start | bytes 3145732
  7.2 26.2 %copy-start.8 = (bf16[512,512]{1,0:T(8,128)(2,1)S(1)}, bf16[512,512]{1,0:T(8,128)(2,1)}, u32[]{:S(2)}) copy-start(bf16[512,512]{1,0:T(8,128)(2,1)} %param.15) | copy-start | bytes 1572868
  7.2 25.3 %copy-start.5 = (bf16[512,512]{1,0:T(8,128)(2,1)S(1)}, bf16[512,512]{1,0:T(8,128)(2,1)}, u32[]{:S(2)}) copy-start(bf16[512,512]{1,0:T(8,128)(2,1)} %param.23) | copy-start | bytes 1572868
  7.2 26.1 %copy-start.2 = (bf16[512,512]{1,0:T(8,128)(2,1)S(1)}, bf16[512,512]{1,0:T(8,128)(2,1)}, u32[]{:S(2)}) copy-start(bf16[512,512]{1,0:T(8,128)(2,1)} %param.14) | copy-start | bytes 1572868
  7.2 29.9 %copy-start.102 = (s32[32,2]{0,1:T(2,128)S(1)}, s32[32,2]{0,1:T(2,128)}, u32[]{:S(2)}) copy-start(s32[32,2]{0,1:T(2,128)} %param.21) | copy-start | bytes 772
  7.2 85.7 %all-gather.9.cloned.1.call-start = ((), (), s32[]{:S(2)}) async-start(), calls=%async_computation.5 | async-start | bytes 8650752 | tf_op jit(solution)/shard_map/all_gather | solution.py:13
  15.2 193.2 %all-gather.11.cloned.1.call-start = ((), (), s32[]{:S(2)}) async-start(), calls=%async_computation.6 | async-start | bytes 34603008 | tf_op jit(solution)/shard_map/all_gather | solution.py:13
  17.8 361.3 %all-reduce.3.cloned.1.call-start = ((), (), s32[]{:S(2)}) async-start(), calls=%async_computation.2 | async-start | bytes 524288 | tf_op jit(solution)/shard_map/psum | solution.py:258
  17.8 305.4 %collective-permute-start.3 = (bf16[512,512]{1,0:T(8,128)(2,1)}, bf16[512,512]{1,0:T(8,128)(2,1)}, u32[]{:S(2)}, u32[]{:S(2)}) collective-permute-start(bf16[512,512]{1,0:T(8,128)(2,1)} %param.16), channel_id=1, source_target_pairs={{0,8},{4,12},{8,16},{12,20},{16,24},{20,28},{24,32},{28,36},{32,40... | collective-permute-start | bytes 1572872 | tf_op jit(solution)/shard_map/ppermute | solution.py:31
  22.2 303.4 %collective-permute-start.2 = (bf16[512,512]{1,0:T(8,128)(2,1)}, bf16[512,512]{1,0:T(8,128)(2,1)}, u32[]{:S(2)}, u32[]{:S(2)}) collective-permute-start(bf16[512,512]{1,0:T(8,128)(2,1)} %param.16), channel_id=1, source_target_pairs={{0,4},{4,8},{8,12},{12,16},{16,20},{20,24},{24,28},{28,32},{32,36}... | collective-permute-start | bytes 1572872 | tf_op jit(solution)/shard_map/ppermute | solution.py:31
  24.4 36.2 %collective-permute-start.1 = (bf16[512,512]{1,0:T(8,128)(2,1)}, bf16[512,512]{1,0:T(8,128)(2,1)}, u32[]{:S(2)}, u32[]{:S(2)}) collective-permute-start(bf16[512,512]{1,0:T(8,128)(2,1)} %param.15), channel_id=1, source_target_pairs={{0,8},{4,12},{8,16},{12,20},{16,24},{20,28},{24,32},{28,36},{32,40... | collective-permute-start | bytes 1572872 | tf_op jit(solution)/shard_map/ppermute | solution.py:31
  27.5 23.8 %collective-permute-start = (bf16[512,512]{1,0:T(8,128)(2,1)}, bf16[512,512]{1,0:T(8,128)(2,1)}, u32[]{:S(2)}, u32[]{:S(2)}) collective-permute-start(bf16[512,512]{1,0:T(8,128)(2,1)} %param.15), channel_id=1, source_target_pairs={{0,4},{4,8},{8,12},{12,16},{16,20},{20,24},{24,28},{28,32},{32,36}... | collective-permute-start | bytes 1572872 | tf_op jit(solution)/shard_map/ppermute | solution.py:31
  32.5 254.0 %copy-start.96 = (pred[128]{0:T(512)(128)(4,1)}, pred[128]{0:T(512)(128)(4,1)S(1)}, u32[]{:S(2)}) copy-start(pred[128]{0:T(512)(128)(4,1)S(1)} %compare_and_fusion) | copy-start | bytes 388
  40.0 246.6 %copy-start.63 = (bf16[128,512]{0,1:T(8,128)(2,1)}, bf16[128,512]{0,1:T(8,128)(2,1)S(1)}, u32[]{:S(2)}) copy-start(bf16[128,512]{0,1:T(8,128)(2,1)S(1)} %copy.137) | copy-start | bytes 393220
  339.5 95.1 %all-gather.13.cloned.1.call-start = ((), (), s32[]{:S(2)}) async-start(), calls=%async_computation.7 | async-start | bytes 8650752 | tf_op jit(solution)/shard_map/all_gather | solution.py:13
  341.3 239.8 %all-gather.15.cloned.1.call-start = ((), (), s32[]{:S(2)}) async-start(), calls=%async_computation.8 | async-start | bytes 34603008 | tf_op jit(solution)/shard_map/all_gather | solution.py:13
  381.7 361.8 %reduce-scatter.3.cloned.1.call-start = ((), (), s32[]{:S(2)}) async-start(), calls=%async_computation.3 | async-start | bytes 1310720 | tf_op jit(solution)/shard_map/reduce_scatter | solution.py:278
  484.2 252.3 %collective-permute-start.4 = (f32[512,512]{0,1:T(8,128)}, f32[512,512]{0,1:T(8,128)}, u32[]{:S(2)}, u32[]{:S(2)}) collective-permute-start(f32[512,512]{0,1:T(8,128)} %pad_maximum_fusion.1), channel_id=1, source_target_pairs={{4,0},{8,4},{12,8},{16,12},{20,16},{24,20},{28,24},{32,28},{36,32}... | collective-permute-start | bytes 3145736 | tf_op jit(solution)/shard_map/ppermute | solution.py:31
  491.0 233.9 %collective-permute-start.7 = (f32[512,512]{0,1:T(8,128)}, f32[512,512]{0,1:T(8,128)}, u32[]{:S(2)}, u32[]{:S(2)}) collective-permute-start(f32[512,512]{0,1:T(8,128)} %pad_maximum_fusion.4), channel_id=1, source_target_pairs={{8,0},{12,4},{16,8},{20,12},{24,16},{28,20},{32,24},{36,28},{40,32... | collective-permute-start | bytes 3145736 | tf_op jit(solution)/shard_map/ppermute | solution.py:31
  686.7 108.4 %reduce-scatter.5.cloned.1.call-start = ((), (), s32[]{:S(2)}) async-start(), calls=%async_computation.4 | async-start | bytes 2162688 | tf_op jit(solution)/shard_map/reduce_scatter | solution.py:254
  689.1 35.8 %collective-permute-start.6 = (f32[512,512]{0,1:T(8,128)}, f32[512,512]{0,1:T(8,128)}, u32[]{:S(2)}, u32[]{:S(2)}) collective-permute-start(f32[512,512]{0,1:T(8,128)} %pad_maximum_fusion.3), channel_id=1, source_target_pairs={{4,0},{8,4},{12,8},{16,12},{20,16},{24,20},{28,24},{32,28},{36,32}... | collective-permute-start | bytes 3145736 | tf_op jit(solution)/shard_map/ppermute | solution.py:31
  696.7 24.5 %copy-start.98 = (s32[128]{0:T(128)S(1)}, s32[128]{0:T(128)}, u32[]{:S(2)}) copy-start(s32[128]{0:T(128)} %copy-done.97) | copy-start | bytes 1540
  711.6 28.4 %collective-permute-start.5 = (f32[512,512]{0,1:T(8,128)}, f32[512,512]{0,1:T(8,128)}, u32[]{:S(2)}, u32[]{:S(2)}) collective-permute-start(f32[512,512]{0,1:T(8,128)} %pad_maximum_fusion.2), channel_id=1, source_target_pairs={{8,0},{12,4},{16,8},{20,12},{24,16},{28,20},{32,24},{36,28},{40,32... | collective-permute-start | bytes 3145736 | tf_op jit(solution)/shard_map/ppermute | solution.py:31
  728.0 67.1 %copy-start.1 = (bf16[512,1024]{1,0:T(8,128)(2,1)S(1)}, bf16[512,1024]{1,0:T(8,128)(2,1)}, u32[]{:S(2)}) copy-start(bf16[512,1024]{1,0:T(8,128)(2,1)} %param.18) | copy-start | bytes 3145732
  (94 other events, 745.7 us)
Sparse Core Ops, SparseCore 0:
  15.4 77.4 all-gather.8
  95.1 113.3 all-gather.10
  339.6 39.4 all-reduce.2
  381.2 53.2 all-gather.12
  436.7 144.4 all-gather.14
  686.9 25.3 reduce-scatter.2
  716.3 78.7 reduce-scatter.4
where the time goes:
time: 812 us; the launch traced here: 802 us
  waiting for transfers between devices  365 us (45%)
  matrix products  281 us (35%)
  local copies, waits for them, and re-layouts  66.5 us (8%)
  other arithmetic  29.6 us (4%)
  blocking collectives  21.1 us (3%)
  starting transfers between devices  19.5 us (2%)
  between operations  17.7 us (2%)
    all_gather x4, waiting for transfers between devices, entering(): pieces = jax.tree.map(lambda part: lax.all_gather(part, axis), value)  274 us
    dot_general x62, matrix products, compose(): jnp.einsum('hab,hbf->haf', later_map[0], earlier_map[1], precision=highest)  150 us
    reduce_scatter x1, waiting for transfers between devices, on_device(): lax.psum_scatter(readout_term, 'ctx', scatter_dimension=0, tiled=True)  49.8 us
    psum x1, waiting for transfers between devices, on_device(): grad_hidden = lax.psum(hidden_term, 'head')  37.8 us
    rev x2, local copies, waits for them, and re-layouts, entering(): pieces = jax.tree.map(lambda part: part[::-1], pieces)  31.3 us
    dot_general x16, matrix products, score_block(): lax.dot_general(left_rows, right_rows, (((1,), (1,)), ((), ())), preferre...  30.4 us
    dot_general x16, matrix products, block_all(): lax.dot_general(grad_scores, queries_tile, (((0,), (0,)), ((), ())), pref...  22.2 us
    psum x1, blocking collectives, on_device(): hidden_read = lax.psum(partial_read, 'head').astype(jnp.bfloat16)  21.1 us
  transfers between devices with their start and end apart: 15, of which 7 were waited for; matrix products, arithmetic and copies ran while one was open for 44% of the time, Pallas kernels for 0%

commit v1 on v0

--- a/solution.py
+++ b/solution.py
@@ -1,11 +1,27 @@
+import functools
 from functools import reduce
 import jax
 import jax.numpy as jnp
 from jax import lax
 from jax.sharding import PartitionSpec as P
+from jax.lax import axis_size, ppermute
 
 masked_score = -1e30
 highest = lax.Precision.HIGHEST
+
+
+def cut_loops(content, peer_axis):
+    count_all = axis_size(peer_axis)
+    met_up = content
+    for dev_j in [
+        [(h, h ^ kk) for h in range(count_all)] for kk in (1, 2, 4, 8, 16) if kk < count_all
+    ]:
+        v_next = ppermute(met_up, peer_axis, perm=dev_j)
+        met_up = met_up + v_next
+    return met_up
+
+
+seats_all_see = functools.partial(cut_loops, peer_axis="head")
 
 
 def entering(value, axis, join, neutral, backward):
@@ -255,7 +271,7 @@
     hidden_term = lax.dot_general(
         grad_memory, readout, (((1,), (1,)), ((), ())), preferred_element_type=jnp.float32
     )
-    grad_hidden = lax.psum(hidden_term, "head")
+    grad_hidden = seats_all_see(hidden_term)
     grad_picked = jnp.einsum("nf,haf->nha", grad_hidden, memory_in, precision=highest).reshape(
         mem_rows, local_heads * head_width
     )

time: 812 us -> 732 us (0.901)
  waiting for transfers between devices: 365 us -> 285 us
    all_gather x4, waiting for transfers between devices: 274 us -> 215 us  [entering(): pieces = jax.tree.map(lambda part: lax.all_gather(part, axis), value)]
    psum x1 -> x0, waiting for transfers between devices: 37.8 us -> none  [on_device(): grad_hidden = lax.psum(hidden_term, 'head')]
    ppermute x0 -> x2, waiting for transfers between devices: none -> 16.7 us  [cut_loops(): v_next = ppermute(met_up, peer_axis, perm=dev_j)]
    unnamed x216 -> x220, local copies, waits for them, and re-layouts: 18.7 us -> 18.9 us
  transfers between devices with their start and end apart: 15 -> 16, of which waited for: 7 -> 7; matrix products, arithmetic and copies ran while one was open for 44% -> 50% of each run, Pallas kernels for 0% -> 0%
where the time goes in v1:
time: 732 us; the launch traced here: 722 us
  waiting for transfers between devices  285 us (39%)
  matrix products  279 us (38%)
  local copies, waits for them, and re-layouts  67.3 us (9%)
  other arithmetic  29.4 us (4%)
  blocking collectives  21.1 us (3%)
  starting transfers between devices  19.8 us (3%)
  between operations  17.9 us (2%)
    all_gather x4, waiting for transfers between devices, entering(): pieces = jax.tree.map(lambda part: lax.all_gather(part, axis), value)  215 us
    dot_general x62, matrix products, compose(): jnp.einsum('hab,hbf->haf', later_map[0], earlier_map[1], precision=highest)  150 us
    reduce_scatter x1, waiting for transfers between devices, on_device(): lax.psum_scatter(readout_term, 'ctx', scatter_dimension=0, tiled=True)  49.7 us
    rev x2, local copies, waits for them, and re-layouts, entering(): pieces = jax.tree.map(lambda part: part[::-1], pieces)  31.8 us
    dot_general x16, matrix products, score_block(): lax.dot_general(left_rows, right_rows, (((1,), (1,)), ((), ())), preferre...  30.5 us
    dot_general x16, matrix products, block_all(): lax.dot_general(grad_scores, queries_tile, (((0,), (0,)), ((), ())), pref...  21.7 us
    psum x1, blocking collectives, on_device(): hidden_read = lax.psum(partial_read, 'head').astype(jnp.bfloat16)  21.1 us
    unnamed x220, local copies, waits for them, and re-layouts  18.9 us
  transfers between devices with their start and end apart: 16, of which 7 were waited for; matrix products, arithmetic and copies ran while one was open for 50% of the time, Pallas kernels for 0%

profile of v1, /device:TPU:0, one launch (start us, length us, event | category | flops | bytes accessed | tf_op | source)
XLA Modules:
  0.0 722.2 jit_solution(18244252271917710028)
XLA Ops:
  17.8 4.3 collective-permute-start.3
  24.4 3.1 collective-permute-start.1
  27.5 3.7 collective-permute-start
  46.4 2.7 fusion.315
  49.1 2.8 fusion.319
  54.1 2.8 fusion.317
  61.3 2.8 fusion.312
  64.0 2.8 fusion.316
  69.6 2.8 fusion.324
  72.3 20.5 %all-gather.9.cloned.1.call-done = f32[128,128,128]{2,1,0:T(8,128)} async-done(((f32[4,128,128]{2,1,0:T(8,128)}), f32[128,128,128]{2,1,0:T(8,128)}) %all-gather.9.cloned.1.call-update) | async-done | bytes 8388624 | tf_op jit(solution)/shard_map/all_gather | solution.py:29
  92.8 115.6 %all-gather.11.cloned.1.call-done = f32[128,128,512]{2,1,0:T(8,128)} async-done(((f32[4,128,512]{2,1,0:T(8,128)}), f32[128,128,512]{2,1,0:T(8,128)}) %all-gather.11.cloned.1.call-update) | async-done | bytes 33554448 | tf_op jit(solution)/shard_map/all_gather | solution.py:29
  208.5 78.4 %while.28 = (s32[]{:T(128)}, f32[4,128,512]{2,1,0:T(8,128)S(1)}, s32[]{:T(128)}, f32[32,4,128,128]{3,2,1,0:T(8,128)}, f32[32,4,128,512]{3,2,1,0:T(8,128)}, /*index=5*/s32[]{:T(128)}, s32[]{:T(128)}) while((s32[]{:T(128)}, f32[4,128,512]{2,1,0:T(8,128)S(1)}, s32[]{:T(128)}, f32[32,4,128,128]{3,2,1,0:T(8,128)}, ...), condition=%wide.region_1.2_spmd.clone, body=%wide.region_0.1_spmd.clone.sunk | while | flops 403701760 | bytes 6556263 | solution.py:41
  288.2 21.1 %all-reduce.1 = bf16[128,512]{1,0:T(8,128)(2,1)S(1)} all-reduce(f32[128,512]{1,0:T(8,128)} %convolution_bitcast_fusion.1), channel_id=1, replica_groups=mesh['ctx'=32,'head'=4] {'head'}, use_global_device_ids=true, to_apply=%region_2.3 | all-reduce | flops 65536 | bytes 393216 | tf_op jit(solution)/shard_map/psum | solution.py:148
  340.7 9.1 %collective-permute-done.4 = f32[128,512]{1,0:T(8,128)S(1)} collective-permute-done((f32[128,512]{1,0:T(8,128)S(1)}, f32[128,512]{1,0:T(8,128)S(1)}, u32[]{:S(2)}, u32[]{:S(2)}) %collective-permute-start.4) | collective-permute-done | bytes 262176 | tf_op jit(solution)/shard_map/ppermute | solution.py:19
  350.1 7.7 %collective-permute-done.5 = f32[128,512]{1,0:T(8,128)S(1)} collective-permute-done((f32[128,512]{1,0:T(8,128)S(1)}, f32[128,512]{1,0:T(8,128)S(1)}, u32[]{:S(2)}, u32[]{:S(2)}) %collective-permute-start.5) | collective-permute-done | bytes 262176 | tf_op jit(solution)/shard_map/ppermute | solution.py:19
  360.1 8.4 %rev.6 = f32[32,4,128,128]{3,2,1,0:T(8,128)} reverse(f32[32,4,128,128]{3,2,1,0:T(8,128)} %bitcast.228), dimensions={0} | reverse | bytes 16777216 | tf_op jit(solution)/shard_map/rev | solution.py:31
  422.2 79.2 %all-gather.15.cloned.1.call-done = f32[128,128,512]{2,1,0:T(8,128)} async-done(((f32[4,128,512]{2,1,0:T(8,128)}), f32[128,128,512]{2,1,0:T(8,128)}) %all-gather.15.cloned.1.call-update) | async-done | bytes 33554448 | tf_op jit(solution)/shard_map/all_gather | solution.py:29
  501.3 23.4 %rev.7 = f32[32,4,128,512]{3,2,1,0:T(8,128)} reverse(f32[32,4,128,512]{3,2,1,0:T(8,128)} %bitcast.227), dimensions={0} | reverse | bytes 67108864 | tf_op jit(solution)/shard_map/rev | solution.py:31
  524.7 78.1 %while.29 = (s32[]{:T(128)}, f32[4,128,512]{2,1,0:T(8,128)S(1)}, s32[]{:T(128)}, f32[32,4,128,128]{3,2,1,0:T(8,128)}, f32[32,4,128,512]{3,2,1,0:T(8,128)}, /*index=5*/s32[]{:T(128)}, s32[]{:T(128)}) while((s32[]{:T(128)}, f32[4,128,512]{2,1,0:T(8,128)S(1)}, s32[]{:T(128)}, f32[32,4,128,128]{3,2,1,0:T(8,128)}, ...), condition=%wide.region_41.42_spmd.clone, body=%wide.region_40.41_spmd.clone.sunk | while | flops 403701760 | bytes 6556263 | solution.py:41
  602.9 4.0 fusion.42
  641.3 3.7 scatter_fusion
  645.0 3.2 fusion.97
  656.7 3.4 collective-permute-done.7
  665.5 49.7 %reduce-scatter.5.cloned.1.call-done = f32[16,1024]{1,0:T(8,128)} async-done(((f32[512,1024]{1,0:T(8,128)}), f32[16,1024]{1,0:T(8,128)}) %reduce-scatter.5.cloned.1.call-update) | async-done | bytes 65552 | tf_op jit(solution)/shard_map/reduce_scatter | solution.py:270
  (528 shorter events, 325.4 us)
Async XLA Ops:
  7.2 302.1 %copy-start = (bf16[512,1024]{1,0:T(8,128)(2,1)S(1)}, bf16[512,1024]{1,0:T(8,128)(2,1)}, u32[]{:S(2)}) copy-start(bf16[512,1024]{1,0:T(8,128)(2,1)} %param.18) | copy-start | bytes 3145732
  7.2 26.0 %copy-start.8 = (bf16[512,512]{1,0:T(8,128)(2,1)S(1)}, bf16[512,512]{1,0:T(8,128)(2,1)}, u32[]{:S(2)}) copy-start(bf16[512,512]{1,0:T(8,128)(2,1)} %param.15) | copy-start | bytes 1572868
  7.2 25.9 %copy-start.2 = (bf16[512,512]{1,0:T(8,128)(2,1)S(1)}, bf16[512,512]{1,0:T(8,128)(2,1)}, u32[]{:S(2)}) copy-start(bf16[512,512]{1,0:T(8,128)(2,1)} %param.14) | copy-start | bytes 1572868
  7.2 29.7 %copy-start.5 = (bf16[512,512]{1,0:T(8,128)(2,1)S(1)}, bf16[512,512]{1,0:T(8,128)(2,1)}, u32[]{:S(2)}) copy-start(bf16[512,512]{1,0:T(8,128)(2,1)} %param.23) | copy-start | bytes 1572868
  7.2 30.5 %copy-start.103 = (s32[32,2]{0,1:T(2,128)S(1)}, s32[32,2]{0,1:T(2,128)}, u32[]{:S(2)}) copy-start(s32[32,2]{0,1:T(2,128)} %param.21) | copy-start | bytes 772
  7.2 85.6 %all-gather.9.cloned.1.call-start = ((), (), s32[]{:S(2)}) async-start(), calls=%async_computation.4 | async-start | bytes 8650752 | tf_op jit(solution)/shard_map/all_gather | solution.py:29
  15.2 193.2 %all-gather.11.cloned.1.call-start = ((), (), s32[]{:S(2)}) async-start(), calls=%async_computation.5 | async-start | bytes 34603008 | tf_op jit(solution)/shard_map/all_gather | solution.py:29
  17.8 342.3 %all-gather.13.cloned.1.call-start = ((), (), s32[]{:S(2)}) async-start(), calls=%async_computation.6 | async-start | bytes 8650752 | tf_op jit(solution)/shard_map/all_gather | solution.py:29
  17.8 304.9 %collective-permute-start.3 = (bf16[512,512]{1,0:T(8,128)(2,1)}, bf16[512,512]{1,0:T(8,128)(2,1)}, u32[]{:S(2)}, u32[]{:S(2)}) collective-permute-start(bf16[512,512]{1,0:T(8,128)(2,1)} %param.16), channel_id=1, source_target_pairs={{0,8},{4,12},{8,16},{12,20},{16,24},{20,28},{24,32},{28,36},{32,40... | collective-permute-start | bytes 1572872 | tf_op jit(solution)/shard_map/ppermute | solution.py:47
  22.1 302.2 %collective-permute-start.2 = (bf16[512,512]{1,0:T(8,128)(2,1)}, bf16[512,512]{1,0:T(8,128)(2,1)}, u32[]{:S(2)}, u32[]{:S(2)}) collective-permute-start(bf16[512,512]{1,0:T(8,128)(2,1)} %param.16), channel_id=1, source_target_pairs={{0,4},{4,8},{8,12},{12,16},{16,20},{20,24},{24,28},{28,32},{32,36}... | collective-permute-start | bytes 1572872 | tf_op jit(solution)/shard_map/ppermute | solution.py:47
  24.4 36.9 %collective-permute-start.1 = (bf16[512,512]{1,0:T(8,128)(2,1)}, bf16[512,512]{1,0:T(8,128)(2,1)}, u32[]{:S(2)}, u32[]{:S(2)}) collective-permute-start(bf16[512,512]{1,0:T(8,128)(2,1)} %param.15), channel_id=1, source_target_pairs={{0,8},{4,12},{8,16},{12,20},{16,24},{20,28},{24,32},{28,36},{32,40... | collective-permute-start | bytes 1572872 | tf_op jit(solution)/shard_map/ppermute | solution.py:47
  27.5 24.4 %collective-permute-start = (bf16[512,512]{1,0:T(8,128)(2,1)}, bf16[512,512]{1,0:T(8,128)(2,1)}, u32[]{:S(2)}, u32[]{:S(2)}) collective-permute-start(bf16[512,512]{1,0:T(8,128)(2,1)} %param.15), channel_id=1, source_target_pairs={{0,4},{4,8},{8,12},{12,16},{16,20},{20,24},{24,28},{28,32},{32,36}... | collective-permute-start | bytes 1572872 | tf_op jit(solution)/shard_map/ppermute | solution.py:47
  33.0 468.3 %all-gather.15.cloned.1.call-start = ((), (), s32[]{:S(2)}) async-start(), calls=%async_computation.7 | async-start | bytes 34603008 | tf_op jit(solution)/shard_map/all_gather | solution.py:29
  33.2 253.7 %copy-start.89 = (pred[128]{0:T(512)(128)(4,1)}, pred[128]{0:T(512)(128)(4,1)S(1)}, u32[]{:S(2)}) copy-start(pred[128]{0:T(512)(128)(4,1)S(1)} %compare_and_fusion) | copy-start | bytes 388
  40.6 246.4 %copy-start.63 = (bf16[128,512]{0,1:T(8,128)(2,1)}, bf16[128,512]{0,1:T(8,128)(2,1)S(1)}, u32[]{:S(2)}) copy-start(bf16[128,512]{0,1:T(8,128)(2,1)S(1)} %copy.137) | copy-start | bytes 393220
  340.6 9.2 %collective-permute-start.4 = (f32[128,512]{1,0:T(8,128)S(1)}, f32[128,512]{1,0:T(8,128)S(1)}, u32[]{:S(2)}, u32[]{:S(2)}) collective-permute-start(f32[128,512]{1,0:T(8,128)S(1)} %fusion.328), channel_id=1, source_target_pairs={{0,1},{1,0},{2,3},{3,2},{4,5},{5,4},{6,7},{7,6},{8,9},{9,8},{10,11... | collective-permute-start | bytes 786440 | tf_op jit(solution)/shard_map/ppermute | solution.py:19
  349.8 8.0 %collective-permute-start.5 = (f32[128,512]{1,0:T(8,128)S(1)}, f32[128,512]{1,0:T(8,128)S(1)}, u32[]{:S(2)}, u32[]{:S(2)}) collective-permute-start(f32[128,512]{1,0:T(8,128)S(1)} %add.328), channel_id=1, source_target_pairs={{0,2},{1,3},{2,0},{3,1},{4,6},{5,7},{6,4},{7,5},{8,10},{9,11},{10,... | collective-permute-start | bytes 786440 | tf_op jit(solution)/shard_map/ppermute | solution.py:19
  359.4 304.2 %reduce-scatter.3.cloned.1.call-start = ((), (), s32[]{:S(2)}) async-start(), calls=%async_computation.2 | async-start | bytes 1310720 | tf_op jit(solution)/shard_map/reduce_scatter | solution.py:294
  409.8 246.9 %collective-permute-start.6 = (f32[512,512]{0,1:T(8,128)}, f32[512,512]{0,1:T(8,128)}, u32[]{:S(2)}, u32[]{:S(2)}) collective-permute-start(f32[512,512]{0,1:T(8,128)} %pad_maximum_fusion.1), channel_id=1, source_target_pairs={{4,0},{8,4},{12,8},{16,12},{20,16},{24,20},{28,24},{32,28},{36,32}... | collective-permute-start | bytes 3145736 | tf_op jit(solution)/shard_map/ppermute | solution.py:47
  416.6 228.4 %collective-permute-start.9 = (f32[512,512]{0,1:T(8,128)}, f32[512,512]{0,1:T(8,128)}, u32[]{:S(2)}, u32[]{:S(2)}) collective-permute-start(f32[512,512]{0,1:T(8,128)} %pad_maximum_fusion.4), channel_id=1, source_target_pairs={{8,0},{12,4},{16,8},{20,12},{24,16},{28,20},{32,24},{36,28},{40,32... | collective-permute-start | bytes 3145736 | tf_op jit(solution)/shard_map/ppermute | solution.py:47
  606.9 108.2 %reduce-scatter.5.cloned.1.call-start = ((), (), s32[]{:S(2)}) async-start(), calls=%async_computation.3 | async-start | bytes 2162688 | tf_op jit(solution)/shard_map/reduce_scatter | solution.py:270
  609.2 35.8 %collective-permute-start.8 = (f32[512,512]{0,1:T(8,128)}, f32[512,512]{0,1:T(8,128)}, u32[]{:S(2)}, u32[]{:S(2)}) collective-permute-start(f32[512,512]{0,1:T(8,128)} %pad_maximum_fusion.3), channel_id=1, source_target_pairs={{4,0},{8,4},{12,8},{16,12},{20,16},{24,20},{28,24},{32,28},{36,32}... | collective-permute-start | bytes 3145736 | tf_op jit(solution)/shard_map/ppermute | solution.py:47
  631.7 28.4 %collective-permute-start.7 = (f32[512,512]{0,1:T(8,128)}, f32[512,512]{0,1:T(8,128)}, u32[]{:S(2)}, u32[]{:S(2)}) collective-permute-start(f32[512,512]{0,1:T(8,128)} %pad_maximum_fusion.2), channel_id=1, source_target_pairs={{8,0},{12,4},{16,8},{20,12},{24,16},{28,20},{32,24},{36,28},{40,32... | collective-permute-start | bytes 3145736 | tf_op jit(solution)/shard_map/ppermute | solution.py:47
  648.2 66.9 %copy-start.1 = (bf16[512,1024]{1,0:T(8,128)(2,1)S(1)}, bf16[512,1024]{1,0:T(8,128)(2,1)}, u32[]{:S(2)}) copy-start(bf16[512,1024]{1,0:T(8,128)(2,1)} %param.18) | copy-start | bytes 3145732
  (97 other events, 919.5 us)
Sparse Core Ops, SparseCore 0:
  15.3 77.4 all-gather.8
  95.1 113.3 all-gather.10
  210.7 52.0 all-gather.12
  359.6 141.7 all-gather.14
  607.0 25.2 reduce-scatter.2
  636.3 78.7 reduce-scatter.4
